TPU v7x, 32 devices: a whole 2x2x4 slice. The times are simulated.
32 devices in a mesh: dp: 16 (over z, y, x), shard: 2 (over core).
Axes of the slice: x: 2, y: 2, z: 4, core: 2. Of those that a mesh axis runs over, the one named last changes fastest.
Arguments:
- acts: bfloat16 [4096, 2048], P('dp', 'shard'), may hold values from -6 to 6
- cotangents: bfloat16 [4096, 2048], P('dp'), may hold values from -6 to 6
- basis_old: float32 [2048, 256], P('shard'), may hold values from -0.125 to 0.125
- moment_first: float32 [2048, 256], P('shard'), may hold values from -4 to 4
- moment_second: float32 [2048, 256], P('shard'), may hold values from 0.05 to 1
Outputs:
- weight_step: float32 [2048, 2048], P('shard')
- basis_new: float32 [2048, 256], P('shard')
- first_new: float32 [2048, 256], P('shard')
- second_new: float32 [2048, 256], P('shard')
All inputs are finite; a program needn't handle non-finite values.
Results may differ from a plain program's by a relative error of at most 0.0003.
Values sent between devices are 32-bit elements; how exact they have to be, the bound alone decides.
A program may use at most 64 MiB of HBM per device.

v0:
```python
import math

import jax
import jax.numpy as jnp
from jax import lax
from jax.sharding import PartitionSpec as P

NS_STEPS = 5


def body(acts, cotangents, basis_old, moment_first, moment_second):
    highest = lax.Precision.HIGHEST
    replicas = lax.axis_size("dp")
    inverse = 1.0 / math.sqrt(acts.shape[0] * replicas)
    grad_part = (
        lax.dot_general(
            cotangents, acts, (((0,), (0,)), ((), ())), preferred_element_type=jnp.float32
        )
        * inverse
    )
    image = lax.psum(jnp.dot(grad_part, basis_old, precision=highest), ("dp", "shard"))
    power_part = jnp.dot(grad_part.T, image, precision=highest)
    power = lax.psum(power_part, "dp")
    gram = lax.psum(jnp.dot(power.T, power, precision=highest), "shard")
    scale = jnp.sqrt(jnp.trace(gram))
    ortho = power / scale
    gram = gram / (scale * scale)
    identity = jnp.eye(gram.shape[0], dtype=jnp.float32)
    for step in range(NS_STEPS):
        ortho = 1.5 * ortho - 0.5 * jnp.dot(ortho, gram, precision=highest)
        if step + 1 < NS_STEPS:
            factor = 1.5 * identity - 0.5 * gram
            gram = jnp.dot(jnp.dot(gram, factor, precision=highest), factor, precision=highest)
    proj_part = lax.psum_scatter(
        jnp.dot(grad_part, ortho, precision=highest), "shard", scatter_dimension=0, tiled=True
    )
    projected = lax.psum(proj_part, "dp")
    first_new = 0.9 * moment_first + 0.1 * projected
    second_new = 0.999 * moment_second + 0.001 * projected * projected
    direction = first_new / (1.0 - 0.9**10) / (jnp.sqrt(second_new / (1.0 - 0.999**10)) + 1e-08)
    weight_step = lax.dot_general(
        ortho,
        lax.all_gather(direction, "shard", axis=0, tiled=True),
        (((1,), (1,)), ((), ())),
        precision=highest,
        preferred_element_type=jnp.float32,
    )
    return (weight_step, ortho, first_new, second_new)


def solution(mesh):
    placed = (P("dp", "shard"), P("dp", None), P("shard", None), P("shard", None), P("shard", None))
    return jax.shard_map(
        body,
        mesh=mesh,
        in_specs=placed,
        out_specs=(P("shard", None), P("shard", None), P("shard", None), P("shard", None)),
        check_vma=False,
    )
```

profile of v0, /device:TPU:0, one launch (start us, length us, event | category | flops | bytes accessed | tf_op | source)
XLA Modules:
  0.0 492.3 jit_solution(7074412818640896374)
XLA Ops:
  7.2 1.2 copy-done
  8.4 2.3 fusion.77
  10.7 3.4 copy-done.1
  14.1 8.2 %fusion.4 = f32[2048,256]{1,0:T(8,128)} fusion(f32[1024,256]{1,0:T(8,128)S(1)} %copy-done.3, f32[2048,1024]{1,0:T(8,128)S(1)} %fusion.77), kind=kOutput, calls=%fused_computation.4 | convolution fusion | flops 6444548096 | bytes 11534336 | tf_op jit(solution)/shard_map/dot_general | solution.py:21
  22.4 0.2 all-reduce.7.cloned.1.call-start
  22.6 136.4 %all-reduce.5.cloned.1.call-done = f32[2048,256]{1,0:T(8,128)} async-done(((f32[2048,256]{1,0:T(8,128)}), f32[2048,256]{1,0:T(8,128)}) %all-reduce.5.cloned.1.call-update) | async-done | bytes 2097168 | tf_op jit(solution)/shard_map/psum | solution.py:21
  159.0 17.1 %fusion.2 = f32[1024,256]{1,0:T(8,128)} fusion(f32[2048,256]{1,0:T(8,128)} %all-reduce.5.cloned.1.call-done, f32[2048,1024]{1,0:T(8,128)} %copy-done.1), kind=kOutput, calls=%fused_computation.2 | convolution fusion | flops 6444548096 | bytes 11534336 | tf_op jit(solution)/shard_map/dot_general | solution.py:22
  176.2 0.0 all-reduce.9.cloned.1.call-start
  176.2 110.7 %all-reduce.7.cloned.1.call-done = f32[1024,256]{1,0:T(8,128)} async-done(((f32[1024,256]{1,0:T(8,128)}), f32[1024,256]{1,0:T(8,128)}) %all-reduce.7.cloned.1.call-update) | async-done | bytes 1048592 | tf_op jit(solution)/shard_map/psum | solution.py:23
  286.9 4.1 fusion.78
  291.0 0.3 reduce-scatter.2.cloned.1.call-start
  291.3 17.2 %all-reduce.9.cloned.1.call-done = f32[256,256]{1,0:T(8,128)} async-done(((f32[256,256]{1,0:T(8,128)}), f32[256,256]{1,0:T(8,128)}) %all-reduce.9.cloned.1.call-update) | async-done | bytes 262160 | tf_op jit(solution)/shard_map/psum | solution.py:24
  308.5 1.6 select_reduce_fusion
  310.8 1.4 fusion.24
  312.3 1.4 fusion.23
  313.6 0.4 fusion.22
  314.0 2.8 fusion.13
  316.8 1.0 fusion.12
  317.8 0.4 fusion.21
  318.2 0.4 fusion.20
  318.7 1.0 fusion.11
  319.7 0.4 fusion.19
  320.1 0.4 fusion.18
  320.5 1.0 fusion.10
  321.5 0.4 fusion.17
  321.9 1.0 fusion.9
  322.9 8.5 %fusion = f32[2048,256]{1,0:T(8,128)} fusion(f32[1024,256]{1,0:T(8,128)S(1)} %fusion.9, f32[2048,1024]{1,0:T(8,128)S(1)} %bitcast.25), kind=kOutput, calls=%fused_computation | convolution fusion | flops 6444548096 | bytes 11534336 | tf_op jit(solution)/shard_map/dot_general | solution.py:35
  331.5 10.9 %reduce-scatter.2.cloned.1.call-done = f32[1024,256]{1,0:T(8,128)} async-done(((f32[2048,256]{1,0:T(8,128)}), f32[1024,256]{1,0:T(8,128)}) %reduce-scatter.2.cloned.1.call-update) | async-done | bytes 1048592 | tf_op jit(solution)/shard_map/reduce_scatter | solution.py:34
  342.5 118.9 %all-reduce.11.cloned.1.call-done = f32[1024,256]{1,0:T(8,128)} async-done(((f32[1024,256]{1,0:T(8,128)}), f32[1024,256]{1,0:T(8,128)}) %all-reduce.11.cloned.1.call-update) | async-done | bytes 1048592 | tf_op jit(solution)/shard_map/psum | solution.py:37
  461.4 3.6 add_divide_fusion
  464.9 9.8 %all-gather.2.cloned.1.call-done = f32[2048,256]{1,0:T(8,128)} async-done(((f32[1024,256]{1,0:T(8,128)}), f32[2048,256]{1,0:T(8,128)}) %all-gather.2.cloned.1.call-update) | async-done | bytes 2097168 | tf_op jit(solution)/shard_map/all_gather | solution.py:43
  474.7 10.3 %fusion.79 = f32[1024,2048]{1,0:T(8,128)} fusion(f32[1024,256]{1,0:T(8,128)S(1)} %fusion.9, f32[2048,256]{1,0:T(8,128)} %all-gather.2.cloned.1.call-done), kind=kOutput, calls=%fused_computation.93 | convolution fusion | flops 6442450944 | bytes 11534336 | tf_op jit(solution)/shard_map/dot_general | solution.py:41
  (22 shorter events, 0.3 us)
Async XLA Ops:
  7.2 1.2 copy-start
  7.2 6.9 %copy-start.3 = (f32[1024,256]{1,0:T(8,128)S(1)}, f32[1024,256]{1,0:T(8,128)}, u32[]{:S(2)}) copy-start(f32[1024,256]{1,0:T(8,128)} %param.7) | copy-start | bytes 3145732
  7.2 151.8 %all-reduce.5.cloned.1.call-start = ((), (), s32[]{:S(2)}) async-start(), calls=%async_computation.1 | async-start | bytes 4194304 | tf_op jit(solution)/shard_map/psum | solution.py:21
  10.7 3.4 copy-start.1
  22.4 264.5 %all-reduce.7.cloned.1.call-start = ((), (), s32[]{:S(2)}) async-start(), calls=%async_computation.2 | async-start | bytes 2097152 | tf_op jit(solution)/shard_map/psum | solution.py:23
  176.2 132.3 %all-reduce.9.cloned.1.call-start = ((), (), s32[]{:S(2)}) async-start(), calls=%async_computation.3 | async-start | bytes 524288 | tf_op jit(solution)/shard_map/psum | solution.py:24
  291.0 51.4 %reduce-scatter.2.cloned.1.call-start = ((), (), s32[]{:S(2)}) async-start(), calls=%async_computation.4 | async-start | bytes 3145728 | tf_op jit(solution)/shard_map/reduce_scatter | solution.py:34
  314.0 8.8 %slice-start = ((s8[8388608]{0:T(1024)(128)(4,1)}), s8[4194304]{0:T(1024)(128)(4,1)S(1)}, s32[]{:S(2)}) async-start(s8[8388608]{0:T(1024)(128)(4,1)} %bitcast.24), calls=%async_computation.7 | async-start | bytes 8388608
  316.8 6.1 %slice-start.1 = ((s8[8388608]{0:T(1024)(128)(4,1)}), s8[4194304]{0:T(1024)(128)(4,1)S(1)}, s32[]{:S(2)}) async-start(s8[8388608]{0:T(1024)(128)(4,1)} %bitcast.24), calls=%async_computation.8 | async-start | bytes 8388608
  322.9 151.8 %copy-start.2 = (f32[1024,256]{1,0:T(8,128)}, f32[1024,256]{1,0:T(8,128)S(1)}, u32[]{:S(2)}) copy-start(f32[1024,256]{1,0:T(8,128)S(1)} %fusion.9) | copy-start | bytes 3145732
  322.9 138.4 %copy-start.4 = (f32[1024,256]{1,0:T(8,128)S(1)}, f32[1024,256]{1,0:T(8,128)}, u32[]{:S(2)}) copy-start(f32[1024,256]{1,0:T(8,128)} %param.8) | copy-start | bytes 3145732
  331.5 129.9 %all-reduce.11.cloned.1.call-start = ((), (), s32[]{:S(2)}) async-start(), calls=%async_computation.5 | async-start | bytes 2097152 | tf_op jit(solution)/shard_map/psum | solution.py:37
  342.4 132.3 %all-gather.2.cloned.1.call-start = ((), (), s32[]{:S(2)}) async-start(), calls=%async_computation.6 | async-start | bytes 3145728 | tf_op jit(solution)/shard_map/all_gather | solution.py:43
Sparse Core Ops, SparseCore 0:
  22.5 136.4 all-reduce.4
  176.3 110.5 all-reduce.6
  291.1 17.3 all-reduce.8
  331.6 10.7 reduce-scatter.1
  348.4 112.9 all-reduce.10
  465.1 9.6 all-gather.1
where the time goes:
time: 499 us; the launch traced here: 492 us
  waiting for transfers between devices  404 us (81%)
  matrix products  62.5 us (13%)
  between operations  15.4 us (3%)
  other arithmetic  5.14 us (1%)
    psum x1, waiting for transfers between devices, body(): lax.psum(jnp.dot(grad_part, basis_old, precision=highest), ('dp', 'shard'))  136 us
    psum x1, waiting for transfers between devices, body(): projected = lax.psum(proj_part, 'dp')  119 us
    psum x1, waiting for transfers between devices, body(): power = lax.psum(power_part, 'dp')  111 us
    psum x1, waiting for transfers between devices, body(): gram = lax.psum(jnp.dot(power.T, power, precision=highest), 'shard')  17.2 us
    dot_general x1, matrix products, body(): power_part = jnp.dot(grad_part.T, image, precision=highest)  17.1 us
    reduce_scatter x1, waiting for transfers between devices, body(): lax.psum_scatter(jnp.dot(grad_part, ortho, precision=highest), 'shard', s...  10.9 us
    dot_general x1, matrix products, body(): lax.dot_general(ortho, lax.all_gather(direction, 'shard', axis=0, tiled=T...  10.3 us
  transfers between devices with their start and end apart: 6, of which 6 were waited for; matrix products, arithmetic and copies ran while one was open for 0% of the time, Pallas kernels for 0%

commit v1 on v0

v1 whole, which is shorter than its diff:
```python
import functools
import math

import jax
import jax.numpy as jnp
from jax import lax
from jax.experimental import pallas as pl
from jax.experimental.pallas import tpu as pltpu
from jax.sharding import PartitionSpec as P

NS_STEPS = 5
F32 = jnp.float32
BF16 = jnp.bfloat16
TILE = 256


def split(x):
    hi = x.astype(BF16)
    return hi, (x - hi.astype(F32)).astype(BF16)


def dot(a, b, dims=((1,), (0,))):
    return lax.dot_general(a, b, (dims, ((), ())), preferred_element_type=F32)


def dot3(a, b, dims=((1,), (0,))):
    a_hi, a_lo = split(a)
    b_hi, b_lo = split(b)
    return dot(a_hi, b_hi, dims) + (dot(a_hi, b_lo, dims) + dot(a_lo, b_hi, dims))


def groups(replicas):
    inner = math.gcd(replicas, 4)
    return inner, replicas // inner


def reduce_kernel(
    replicas, shards, pieces,
    acts, cot, basis, first, second,
    power, mix, q_all, first_all, second_all,
    cot_t, acts_t, part, acc, image, recv_inner, recv_outer, tok, tok_recv, gram, gram_recv, ns_g, ns_t,
    dp_send, dp_recv, sh_send, sh_recv, fwd_send, fwd_recv,
):
    inner, outer = groups(replicas)
    me = lax.axis_index("dp")
    own = lax.axis_index("shard")
    at_inner, at_outer = lax.rem(me, inner), lax.div(me, inner)
    tokens, features = acts.shape
    rows = cot.shape[1] // shards
    rank = basis.shape[1]
    width = rank // pieces
    inverse = 1.0 / math.sqrt(tokens * replicas)

    def dp_inner(k):
        return at_outer * inner + lax.rem(at_inner + k, inner)

    def dp_outer(k):
        return lax.rem(at_outer + k, outer) * inner + at_inner

    def remote(src, dst, send, recv, where):
        copy = pltpu.make_async_remote_copy(
            src_ref=src, dst_ref=dst, send_sem=send, recv_sem=recv,
            device_id=where, device_id_type=pl.DeviceIdType.MESH,
        )
        copy.start()
        return copy

    def to_shard(k):
        return (me, lax.rem(own + k, shards))

    barrier = pltpu.get_barrier_semaphore()
    for k in range(1, inner):
        pl.semaphore_signal(barrier, inc=1, device_id=(dp_inner(k), own), device_id_type=pl.DeviceIdType.MESH)
    for k in range(1, outer):
        pl.semaphore_signal(barrier, inc=1, device_id=(dp_outer(k), own), device_id_type=pl.DeviceIdType.MESH)
    for k in range(1, shards):
        pl.semaphore_signal(barrier, inc=1, device_id=to_shard(k), device_id_type=pl.DeviceIdType.MESH)

    def tiles(count, fn):
        step = min(TILE, count)

        def one(i, carry):
            fn(pl.multiple_of(i * step, step), step)
            return carry

        lax.fori_loop(0, count // step, one, 0)

    def transposes(at, n):
        cot_t[pl.ds(at, n), :] = cot[:, pl.ds(pl.multiple_of(own * rows + at, 128), n)].T

    def transposes_acts(at, n):
        acts_t[pl.ds(at, n), :] = acts[:, pl.ds(at, n)].T

    def read(ref, count, at, n):
        return jnp.concatenate([ref[pl.ds(s * count + at, n), :] for s in range(pieces)], axis=1)

    def contract(left, column, ref, count, out):
        out[...] = jnp.zeros_like(out)

        def one(at, n):
            hi, lo = split(read(ref, count, at, n))
            block = left[:, pl.ds(pl.multiple_of(column + at, 128), n)]
            out[...] += dot(block, hi) + dot(block, lo)

        tiles(count, one)

    def expand(left, right, count):
        hi, lo = split(right)

        def one(at, n):
            block = left[pl.ds(at, n), :]
            value = dot(block, hi) + dot(block, lo)
            for s in range(pieces):
                part[pl.ds(s * count + at, n), :] = value[:, s * width : (s + 1) * width]

        tiles(count, one)

    def exchange(index, buffer, received):
        return [
            remote(buffer, received.at[k - 1], sh_send.at[index, k - 1], sh_recv.at[index, k - 1], to_shard(k))
            for k in range(1, shards)
        ]

    def total(copies, buffer, received):
        value = buffer[...]
        for k, copy in enumerate(copies):
            copy.wait()
            value = value + received[k]
        return value

    def reduce_start(index, count):
        chunk = count * pieces // inner
        copies = []
        for k in range(1, inner):
            at = pl.multiple_of(lax.rem(at_inner + k, inner) * chunk, 8)
            copies.append(remote(
                part.at[pl.ds(at, chunk), :], recv_inner.at[index, k - 1],
                dp_send.at[index, 0, k - 1], dp_recv.at[index, 0, k - 1], (dp_inner(k), own),
            ))
        return copies

    def reduce_finish(index, count, full, copies, arrived=None):
        chunk = count * pieces // inner
        small = chunk // outer
        base = pl.multiple_of(at_inner * chunk, 8)
        for copy in copies:
            copy.wait()
        value = part[pl.ds(base, chunk), :]
        for k in range(1, inner):
            value = value + recv_inner[index, k - 1]
        acc[...] = value
        copies = []
        for k in range(1, outer):
            at = pl.multiple_of(lax.rem(at_outer + k, outer) * small, 8)
            copies.append(remote(
                acc.at[pl.ds(at, small), :], recv_outer.at[index, k - 1],
                dp_send.at[index, 1, k - 1], dp_recv.at[index, 1, k - 1], (dp_outer(k), own),
            ))
        for copy in copies:
            copy.wait()
        value = acc[pl.ds(pl.multiple_of(at_outer * small, 8), small), :]
        for k in range(1, outer):
            value = value + recv_outer[index, k - 1]
        mine = pl.ds(pl.multiple_of(base + at_outer * small, 8), small)
        full[mine, :] = value
        copies = [
            remote(
                full.at[mine, :], full.at[mine, :],
                dp_send.at[index, 2, k - 1], dp_recv.at[index, 2, k - 1], (dp_outer(k), own),
            )
            for k in range(1, outer)
        ]
        for copy in copies:
            copy.wait()
        mine = pl.ds(base, chunk)
        copies = [
            remote(
                full.at[mine, :], full.at[mine, :],
                dp_send.at[index, 3, k - 1], dp_recv.at[index, 3, k - 1], (dp_inner(k), own),
            )
            for k in range(1, inner)
        ]
        forwards = []
        if arrived is not None:
            forwards += arrived(0, base, chunk)
        for k, copy in enumerate(copies):
            copy.wait_recv()
            if arrived is not None:
                at = pl.multiple_of(lax.rem(at_inner + inner - k - 1, inner) * chunk, 8)
                forwards += arrived(k + 1, at, chunk)
        for copy in copies:
            copy.wait_send()
        for copy in forwards:
            copy.wait()

    contract(acts, 0, basis, features, tok.at[0]) if pieces == 1 else None
    if pieces > 1:
        tok[0] = jnp.zeros_like(tok[0])

        def one(at, n):
            hi, lo = split(basis[pl.ds(at, n), :])
            block = acts[:, pl.ds(at, n)]
            tok[0] += dot(block, hi) + dot(block, lo)

        tiles(features, one)
    pl.semaphore_wait(barrier, inner + outer + shards - 3)
    copies = exchange(0, tok.at[0], tok_recv.at[0])
    moments = []
    for k in range(1, shards):
        slot = pl.ds((shards - k) * rows, rows)
        moments.append(remote(
            first, first_all.at[slot, :], sh_send.at[4, k - 1], sh_recv.at[4, k - 1], to_shard(k)))
        moments.append(remote(
            second, second_all.at[slot, :], sh_send.at[5, k - 1], sh_recv.at[5, k - 1], to_shard(k)))
    first_all[pl.ds(0, rows), :] = first[...]
    second_all[pl.ds(0, rows), :] = second[...]
    tiles(rows, transposes)
    value = total(copies, tok.at[0], tok_recv.at[0]) * inverse
    expand(cot_t, value, rows)
    copies = reduce_start(0, rows)
    tiles(features, transposes_acts)
    reduce_finish(0, rows, image, copies)

    contract(cot, own * rows, image, rows, tok.at[1])
    copies = exchange(1, tok.at[1], tok_recv.at[1])
    value = total(copies, tok.at[1], tok_recv.at[1]) * inverse
    expand(acts_t, value, features)
    copies = reduce_start(1, features)
    reduce_finish(1, features, power, copies)

    contract(acts, 0, power, features, tok.at[2])
    copies = exchange(2, tok.at[2], tok_recv.at[2])
    gram[...] = jnp.zeros_like(gram)

    def one_gram(at, n):
        hi, lo = split(read(power, features, at, n))
        hi_t = hi.T
        cross = dot(hi_t, lo)
        gram[...] += dot(hi_t, hi) + (cross + cross.T)

    tiles(features, one_gram)
    gram_copies = exchange(3, gram, gram_recv)
    value = total(copies, tok.at[2], tok_recv.at[2]) * inverse
    expand(cot_t, value, rows)
    copies = reduce_start(2, rows)

    g = total(gram_copies, gram, gram_recv)
    diagonal = lax.broadcasted_iota(jnp.int32, g.shape, 0) == lax.broadcasted_iota(jnp.int32, g.shape, 1)
    identity = jnp.where(diagonal, 1.0, 0.0).astype(F32)
    scale = jnp.sqrt(jnp.sum(jnp.where(diagonal, g, 0.0), keepdims=True))
    g = g / (scale * scale)
    ns_g[...] = g
    ns_t[...] = 1.5 * identity - 0.5 * g

    def newton(i, carry):
        g = ns_g[...]
        factor = 1.5 * identity - 0.5 * g
        g = dot3(dot3(g, factor), factor)
        ns_g[...] = g
        ns_t[...] = dot3(ns_t[...], 1.5 * identity - 0.5 * g)
        return carry

    lax.fori_loop(0, NS_STEPS - 1, newton, 0)
    mix[...] = ns_t[...] / scale

    def arrived(j, at, n):
        return [
            remote(
                q_all.at[pl.ds(at, n), :],
                q_all.at[pl.ds(pl.multiple_of((shards - k) * rows * pieces + at, 8), n), :],
                fwd_send.at[j, k - 1], fwd_recv.at[j, k - 1], to_shard(k),
            )
            for k in range(1, shards)
        ]

    reduce_finish(2, rows, q_all, copies, arrived)
    for copy in moments:
        copy.wait()


def finish_kernel(blocks, where, power, mix, q, first, second, step_out, basis_out, first_out, second_out, right):
    j = pl.program_id(0)

    @pl.when(j == 0)
    def _():
        count = power.shape[0]
        tile = min(TILE, count)
        for i in range(count // tile):
            at = pl.ds(i * tile, tile)
            basis_out[at, :] = dot3(power[at, :], mix[...])

    projected = dot3(q[...], mix[...])
    first_new = 0.9 * first[...] + 0.1 * projected
    second_new = 0.999 * second[...] + 0.001 * projected * projected

    @pl.when(j < blocks)
    def _():
        first_out[...] = first_new
        second_out[...] = second_new

    direction = first_new / (1.0 - 0.9**10) / (jnp.sqrt(second_new / (1.0 - 0.999**10)) + 1e-08)
    right[...] = direction.T
    hi, lo = split(right[...])
    count = power.shape[0]
    tile = min(TILE, count)
    for i in range(count // tile):
        at = pl.ds(i * tile, tile)
        a_hi, a_lo = split(basis_out[at, :])
        step_out[at, :] = dot(a_hi, hi) + (dot(a_hi, lo) + dot(a_lo, hi))


def body(replicas, shards, acts, cotangents, basis_old, moment_first, moment_second):
    tokens, features = acts.shape
    outs = cotangents.shape[1]
    rows = outs // shards
    rank = basis_old.shape[1]
    inner, outer = groups(replicas)
    pieces = 1 if min(rows, features) // replicas % 8 == 0 else 2
    width = rank // pieces
    most = max(rows, features) * pieces
    vmem = pl.BlockSpec(memory_space=pltpu.VMEM)
    links = max(inner, outer)
    sem = pltpu.SemaphoreType.DMA
    power, mix, q_all, first_all, second_all = pl.pallas_call(
        functools.partial(reduce_kernel, replicas, shards, pieces),
        out_shape=[
            jax.ShapeDtypeStruct((features * pieces, width), F32),
            jax.ShapeDtypeStruct((rank, rank), F32),
            jax.ShapeDtypeStruct((outs * pieces, width), F32),
            jax.ShapeDtypeStruct((outs, rank), F32),
            jax.ShapeDtypeStruct((outs, rank), F32),
        ],
        in_specs=[vmem] * 5,
        out_specs=[vmem] * 5,
        scratch_shapes=[
            pltpu.VMEM((rows, tokens), BF16),
            pltpu.VMEM((features, tokens), BF16),
            pltpu.VMEM((most, width), F32),
            pltpu.VMEM((most // inner, width), F32),
            pltpu.VMEM((rows * pieces, width), F32),
            pltpu.VMEM((3, inner - 1, most // inner, width), F32),
            pltpu.VMEM((3, outer - 1, most // inner // outer, width), F32),
            pltpu.VMEM((3, tokens, rank), F32),
            pltpu.VMEM((3, shards - 1, tokens, rank), F32),
            pltpu.VMEM((rank, rank), F32),
            pltpu.VMEM((shards - 1, rank, rank), F32),
            pltpu.VMEM((rank, rank), F32),
            pltpu.VMEM((rank, rank), F32),
            sem((3, 4, links)),
            sem((3, 4, links)),
            sem((6, shards)),
            sem((6, shards)),
            sem((inner, shards)),
            sem((inner, shards)),
        ],
        compiler_params=pltpu.CompilerParams(
            collective_id=0, has_side_effects=True, vmem_limit_bytes=48 * 2**20
        ),
    )(acts, cotangents, basis_old, moment_first, moment_second)
    if pieces > 1:
        power = power.reshape(pieces, features, width).transpose(1, 0, 2).reshape(features, rank)
        q_all = q_all.reshape(shards, pieces, rows, width).transpose(0, 2, 1, 3).reshape(outs, rank)

    tile = min(TILE, rows)
    blocks = rows // tile
    where = lax.axis_index("shard").astype(jnp.int32).reshape(1)

    def column(j, at):
        return (0, lax.rem(at[0] + lax.div(j, blocks), shards) * blocks + lax.rem(j, blocks))

    fixed = lambda j, at: (0, 0)
    along = lambda j, at: (j, 0)
    early = lambda j, at: (jnp.minimum(j, blocks - 1), 0)
    return pl.pallas_call(
        functools.partial(finish_kernel, blocks),
        out_shape=[
            jax.ShapeDtypeStruct((features, outs), F32),
            jax.ShapeDtypeStruct((features, rank), F32),
            jax.ShapeDtypeStruct((rows, rank), F32),
            jax.ShapeDtypeStruct((rows, rank), F32),
        ],
        grid_spec=pltpu.PrefetchScalarGridSpec(
            num_scalar_prefetch=1,
            grid=(outs // tile,),
            in_specs=[
                pl.BlockSpec((features, rank), fixed),
                pl.BlockSpec((rank, rank), fixed),
                pl.BlockSpec((tile, rank), along),
                pl.BlockSpec((tile, rank), along),
                pl.BlockSpec((tile, rank), along),
            ],
            out_specs=[
                pl.BlockSpec((features, tile), column),
                pl.BlockSpec((features, rank), fixed),
                pl.BlockSpec((tile, rank), early),
                pl.BlockSpec((tile, rank), early),
            ],
            scratch_shapes=[pltpu.VMEM((rank, tile), F32)],
        ),
        compiler_params=pltpu.CompilerParams(vmem_limit_bytes=48 * 2**20),
    )(where, power, mix, q_all, first_all, second_all)


def solution(mesh):
    placed = (P("dp", "shard"), P("dp", None), P("shard", None), P("shard", None), P("shard", None))
    return jax.shard_map(
        functools.partial(body, mesh.shape["dp"], mesh.shape["shard"]),
        mesh=mesh,
        in_specs=placed,
        out_specs=(P("shard", None), P("shard", None), P("shard", None), P("shard", None)),
        check_vma=False,
    )
```

time: 499 us -> 156 us (0.31); the launches traced: 492 us -> 155 us
  waiting for transfers between devices: 404 us -> 0 us
  Pallas kernels: 0 us -> 145 us
  matrix products: 62.5 us -> 0 us
  between operations: 15.4 us -> 0.67 us
  other arithmetic: 5.14 us -> 0 us
    psum x4 -> x0, waiting for transfers between devices: 383 us -> none  [the longest x1 136 us: body(): lax.psum(jnp.dot(grad_part, basis_old, precision=highest), ('dp', 'shard'))]
    pallas_call x0 -> x2, Pallas kernels: none -> 145 us  [the longest x1 134 us: body(): pl.pallas_call(functools.partial(reduce_kernel, replicas, shards, pieces)...]
    dot_general x19 -> x0, matrix products: 62.5 us -> none  [the longest x1 17.1 us: body(): power_part = jnp.dot(grad_part.T, image, precision=highest)]
    reduce_scatter x1 -> x0, waiting for transfers between devices: 10.9 us -> none  [body(): lax.psum_scatter(jnp.dot(grad_part, ortho, precision=highest), 'shard', s...]
    all_gather x1 -> x0, waiting for transfers between devices: 9.8 us -> none  [body(): lax.all_gather(direction, 'shard', axis=0, tiled=True)]
  transfers between devices with their start and end apart: 6 -> 0, of which waited for: 6 -> 0; matrix products, arithmetic and copies ran while one was open for 0% -> 0% of each run, Pallas kernels for 0% -> 0%
where the time goes in v1:
time: 156 us; the launch traced here: 155 us
  Pallas kernels  145 us (93%)
  local copies, waits for them, and re-layouts  9.11 us (6%)
    pallas_call x1, Pallas kernels, body(): pl.pallas_call(functools.partial(reduce_kernel, replicas, shards, pieces)...  134 us
    pallas_call x1, Pallas kernels, body(): pl.pallas_call(functools.partial(finish_kernel, blocks), out_shape=[jax.S...  11.3 us
    unnamed x14, local copies, waits for them, and re-layouts  9.11 us

profile of v1, /device:TPU:0, one launch (start us, length us, event | category | flops | bytes accessed | tf_op | source)
XLA Modules:
  0.0 155.2 jit_solution(9964885992379448151)
XLA Ops:
  0.6 0.0 copy-start.2
  0.6 1.2 copy-done.2
  1.9 0.0 copy-start.3
  1.9 1.2 copy-done.3
  3.1 0.0 copy-start.4
  3.1 1.2 copy-done.4
  4.3 0.0 copy-start.5
  4.3 1.2 copy-done.5
  5.5 0.0 copy-start.6
  5.5 1.0 copy-done.6
  6.6 134.1 %shard_map.84 = (f32[1024,256]{1,0:T(8,128)S(1)}, f32[256,256]{1,0:T(8,128)S(1)}, f32[2048,256]{1,0:T(8,128)}, f32[2048,256]{1,0:T(8,128)}, f32[2048,256]{1,0:T(8,128)}) custom-call(bf16[256,1024]{1,0:T(8,128)(2,1)S(1)} %copy-done.6, bf16[256,2048]{1,0:T(8,128)(2,1)S(1)} %copy-done.2, f32[1024,256]{1,0:T(8,128)S(1)} %copy-done.3, f32[1024,256]{1,0:T(8,128)S(1)} %copy-done.4, ...), custom_call_target="tpu_custom_call" | custom-call | tf_op jit(solution)/shard_map/pallas_call | solution.py:324
  140.7 0.0 copy-start
  140.7 1.6 %copy-done = f32[2048,256]{1,0:T(8,128)S(1)} copy-done((f32[2048,256]{1,0:T(8,128)S(1)}, f32[2048,256]{1,0:T(8,128)}, u32[]{:S(2)}) %copy-start) | copy-done | bytes 2097176
  142.2 0.0 copy-start.1
  142.3 1.6 %copy-done.1 = f32[2048,256]{1,0:T(8,128)S(1)} copy-done((f32[2048,256]{1,0:T(8,128)S(1)}, f32[2048,256]{1,0:T(8,128)}, u32[]{:S(2)}) %copy-start.1) | copy-done | bytes 2097176
  143.8 11.3 %shard_map.85 = (f32[1024,2048]{1,0:T(8,128)}, f32[1024,256]{1,0:T(8,128)}, f32[1024,256]{1,0:T(8,128)}, f32[1024,256]{1,0:T(8,128)}) custom-call(s32[1]{0:T(128)} %bitcast.where, f32[1024,256]{1,0:T(8,128)S(1)} %get-tuple-element.9.power, f32[256,256]{1,0:T(8,128)S(1)} %get-tuple-element.10.mix, f32[2048,256]{1,0:T(8,128)S(1)} %copy-done, ...), custom_call_target="tpu_custom_call" | custom-call | tf_op jit(solution)/shard_map/pallas_call | solution.py:374
Async XLA Ops:
  0.6 1.2 copy-start.2
  1.9 1.2 copy-start.3
  3.1 1.2 copy-start.4
  4.3 1.2 copy-start.5
  5.5 1.0 copy-start.6
  140.7 1.6 %copy-start = (f32[2048,256]{1,0:T(8,128)S(1)}, f32[2048,256]{1,0:T(8,128)}, u32[]{:S(2)}) copy-start(f32[2048,256]{1,0:T(8,128)} %get-tuple-element.11.q) | copy-start | bytes 6291460
  142.2 1.6 %copy-start.1 = (f32[2048,256]{1,0:T(8,128)S(1)}, f32[2048,256]{1,0:T(8,128)}, u32[]{:S(2)}) copy-start(f32[2048,256]{1,0:T(8,128)} %get-tuple-element.12.first) | copy-start | bytes 6291460

commit v2 on v0

v2 whole, which is shorter than its diff:
```python
import functools
import math

import jax
import jax.numpy as jnp
from jax import lax
from jax.experimental import pallas as pl
from jax.experimental.pallas import tpu as pltpu
from jax.sharding import PartitionSpec as P

NS_STEPS = 5
F32 = jnp.float32
BF16 = jnp.bfloat16
TILE = 256
BLOCKS = 4
WHOLE_VMEM = 62 * 2**20


def split(x):
    hi = x.astype(BF16)
    return hi, (x - hi.astype(F32)).astype(BF16)


def dot(a, b, dims=((1,), (0,))):
    return lax.dot_general(a, b, (dims, ((), ())), preferred_element_type=F32)


def dot3(a, b, dims=((1,), (0,))):
    a_hi, a_lo = split(a)
    b_hi, b_lo = split(b)
    return dot(a_hi, b_hi, dims) + (dot(a_hi, b_lo, dims) + dot(a_lo, b_hi, dims))


def stages(replicas, odd):
    pairs, stride, left = [], 1, replicas
    while left % 2 == 0 and len(pairs) < 2:
        pairs.append((stride, 2))
        stride, left = stride * 2, left // 2
    if odd:
        pairs = pairs[::-1]
    return pairs + [(stride, left)]


def reduce_kernel(
    replicas, shards, pieces, blocks,
    acts_in, cot_in, basis_in, first, second,
    power, mix, q_all, first_all, second_all,
    acts, cot, basis, cot_t, acts_t, part, image, recv_a, recv_b, recv_c, tok, tok_recv, gram, gram_recv, ns_g, ns_t,
    load_sem, dp_send, dp_recv, sh_send, sh_recv, fwd_send, fwd_recv,
):
    me = lax.axis_index("dp")
    own = lax.axis_index("shard")
    tokens, features = acts.shape
    rows = cot.shape[1] // shards
    rank = basis.shape[1]
    width = rank // pieces
    inverse = 1.0 / math.sqrt(tokens * replicas)
    receive = (recv_a, recv_b, recv_c)
    mesh_id = pl.DeviceIdType.MESH

    loads = [
        pltpu.make_async_copy(basis_in, basis, load_sem.at[0]),
        pltpu.make_async_copy(acts_in, acts, load_sem.at[1]),
        pltpu.make_async_copy(cot_in, cot, load_sem.at[2]),
    ]
    for load in loads:
        load.start()

    def place(stride, size):
        return lax.rem(lax.div(me, stride), size)

    def peer(stride, size, k):
        at = place(stride, size)
        return me + (lax.rem(at + k, size) - at) * stride

    def remote(src, dst, send, recv, where):
        copy = pltpu.make_async_remote_copy(
            src_ref=src, dst_ref=dst, send_sem=send, recv_sem=recv,
            device_id=where, device_id_type=mesh_id,
        )
        copy.start()
        return copy

    def to_shard(k):
        return (me, lax.rem(own + k, shards))

    barrier = pltpu.get_barrier_semaphore()
    greeted = 0
    for stride, size in stages(replicas, False):
        for k in range(1, size):
            pl.semaphore_signal(barrier, inc=1, device_id=(peer(stride, size, k), own), device_id_type=mesh_id)
            greeted += 1
    for k in range(1, shards):
        pl.semaphore_signal(barrier, inc=1, device_id=to_shard(k), device_id_type=mesh_id)
        greeted += 1

    def tiles(start, count, fn):
        step = min(TILE, count)
        if count == step:
            fn(start, step)
            return

        def one(i, carry):
            fn(pl.multiple_of(start + i * step, step), step)
            return carry

        lax.fori_loop(0, count // step, one, 0)

    def turn_cot(at, n):
        cot_t[pl.ds(at, n), :] = cot[:, pl.ds(pl.multiple_of(own * rows + at, 128), n)].T

    def turn_acts(at, n):
        acts_t[pl.ds(at, n), :] = acts[:, pl.ds(at, n)].T

    def read(ref, count, at, n):
        if pieces == 1:
            return ref[pl.ds(at, n), :]
        return jnp.concatenate([ref[pl.ds(s * count + at, n), :] for s in range(pieces)], axis=1)

    def contract(left, column, hi, lo, at, n, out, fresh):
        block = left[:, pl.ds(pl.multiple_of(column + at, 128), n)]
        value = dot(block, hi) + dot(block, lo)
        if fresh:
            out[...] = value
        else:
            out[...] += value

    def exchange(index, buffer, received):
        return [
            remote(buffer, received.at[k - 1], sh_send.at[index, k - 1], sh_recv.at[index, k - 1], to_shard(k))
            for k in range(1, shards)
        ]

    def total(copies, buffer, received):
        value = buffer[...]
        for k, copy in enumerate(copies):
            copy.wait()
            value = value + received[k]
        return value

    def piece(index, h, count, left, hi, lo, full, consume):
        length = count * pieces // blocks
        base = h * length

        def expand(at, n):
            block = left[pl.ds(at, n), :]
            value = dot(block, hi) + dot(block, lo)
            for s in range(pieces):
                part[pl.ds(s * count + at, n), :] = value[:, s * width : (s + 1) * width]

        tiles(h * (count // blocks), count // blocks, expand)
        slot = index * blocks + h
        path = stages(replicas, h % 2 == 1)
        for stage, (stride, size) in enumerate(path):
            chunk = length // size
            at = place(stride, size)
            copies = [
                remote(
                    part.at[pl.ds(pl.multiple_of(base + lax.rem(at + k, size) * chunk, 8), chunk), :],
                    receive[stage].at[slot, k - 1],
                    dp_send.at[slot, stage, k - 1], dp_recv.at[slot, stage, k - 1], (peer(stride, size, k), own),
                )
                for k in range(1, size)
            ]
            yield
            base = pl.multiple_of(base + at * chunk, 8)
            length = chunk
            value = part[pl.ds(base, chunk), :]
            for k, copy in enumerate(copies):
                copy.wait()
                value = value + receive[stage][slot, k]
            if stage + 1 < len(path):
                part[pl.ds(base, chunk), :] = value
            else:
                full[pl.ds(base, chunk), :] = value
        for stage, (stride, size) in reversed(list(enumerate(path))):
            mine = full.at[pl.ds(base, length), :]
            copies = [
                remote(
                    mine, mine,
                    dp_send.at[slot, 3 + stage, k - 1], dp_recv.at[slot, 3 + stage, k - 1], (peer(stride, size, k), own),
                )
                for k in range(1, size)
            ]
            yield
            for copy in copies:
                copy.wait()
            base = pl.multiple_of(base - place(stride, size) * length, 8)
            length = length * size
        consume(h)

    def run(index, count, left, value, full, consume, beside=None):
        hi, lo = split(value)
        active = []
        for h in range(blocks):
            active.append(piece(index, h, count, left, hi, lo, full, consume))
            next(active[h])
        if beside is not None:
            active.append(beside())
        while active:
            active = [one for one in active if next(one, one) is None]

    loads[0].wait()
    loads[1].wait()

    def project(at, n):
        hi, lo = split(basis[pl.ds(at, n), :])
        block = acts[:, pl.ds(at, n)]
        tok[0] += dot(block, hi) + dot(block, lo)

    tok[0] = jnp.zeros_like(tok[0])
    tiles(0, features, project)
    loads[2].wait()
    pl.semaphore_wait(barrier, greeted)
    copies = exchange(0, tok.at[0], tok_recv.at[0])
    tiles(0, rows, turn_cot)
    value = total(copies, tok.at[0], tok_recv.at[0]) * inverse
    moments = []

    def early():
        for k in range(1, shards):
            slot = pl.ds((shards - k - 1) * rows, rows)
            moments.append(remote(
                first, first_all.at[slot, :], sh_send.at[4, k - 1], sh_recv.at[4, k - 1], to_shard(k)))
            moments.append(remote(
                second, second_all.at[slot, :], sh_send.at[5, k - 1], sh_recv.at[5, k - 1], to_shard(k)))
        tiles(0, features, turn_acts)
        yield

    def use_image(h):
        def one(at, n):
            hi, lo = split(read(image, rows, at, n))
            contract(cot, own * rows, hi, lo, at, n, tok.at[1], h == 0)

        tiles(h * (rows // blocks), rows // blocks, one)

    run(0, rows, cot_t, value, image, use_image, early)
    copies = exchange(1, tok.at[1], tok_recv.at[1])
    value = total(copies, tok.at[1], tok_recv.at[1]) * inverse

    def use_power(h):
        def one(at, n):
            hi, lo = split(read(power, features, at, n))
            contract(acts, 0, hi, lo, at, n, tok.at[2], h == 0)
            hi_t = hi.T
            cross = dot(hi_t, lo)
            value = dot(hi_t, hi) + (cross + cross.T)
            if h == 0:
                gram[...] = value
            else:
                gram[...] += value

        tiles(h * (features // blocks), features // blocks, one)

    run(1, features, acts_t, value, power, use_power)
    copies = exchange(2, tok.at[2], tok_recv.at[2])
    gram_copies = exchange(3, gram, gram_recv)
    value = total(copies, tok.at[2], tok_recv.at[2]) * inverse

    def newton():
        g = total(gram_copies, gram, gram_recv)
        diagonal = lax.broadcasted_iota(jnp.int32, g.shape, 0) == lax.broadcasted_iota(jnp.int32, g.shape, 1)
        scale = jnp.sqrt(jnp.sum(jnp.where(diagonal, g, 0.0), keepdims=True))
        g = g / (scale * scale)

        def factor_of(g):
            return jnp.where(diagonal, 1.5, 0.0) - 0.5 * g

        ns_g[...] = g
        ns_t[...] = factor_of(g)
        yield
        for _ in range(NS_STEPS - 1):
            factor = factor_of(ns_g[...])
            g = dot3(dot3(ns_g[...], factor), factor)
            ns_g[...] = g
            ns_t[...] = dot3(ns_t[...], factor_of(g))
            yield
        mix[...] = ns_t[...] / scale

    forwards = []

    def pass_on(h):
        n = rows * pieces // blocks
        at = h * n
        for k in range(1, shards):
            forwards.append(remote(
                q_all.at[pl.ds(at, n), :],
                q_all.at[pl.ds((shards - k) * rows * pieces + at, n), :],
                fwd_send.at[h, k - 1], fwd_recv.at[h, k - 1], to_shard(k),
            ))

    run(2, rows, cot_t, value, q_all, pass_on, newton)
    for copy in moments + forwards:
        copy.wait()


def finish_kernel(
    blocks, where, power, mix, q, first, second, first_far, second_far,
    step_out, basis_out, first_out, second_out, basis_hi, basis_lo, mean, square,
):
    j = pl.program_id(0)
    count = power.shape[0]
    tile = min(TILE, count)

    @pl.when(j == 0)
    def _():
        for i in range(count // tile):
            at = pl.ds(i * tile, tile)
            value = dot3(power[at, :], mix[...])
            basis_out[at, :] = value
            hi, lo = split(value)
            basis_hi[at, :] = hi
            basis_lo[at, :] = lo

    projected = dot3(q[...], mix[...])

    def adam(first, second):
        mean[...] = 0.9 * first[...] + 0.1 * projected
        square[...] = 0.999 * second[...] + 0.001 * projected * projected

    @pl.when(j < blocks)
    def _():
        adam(first, second)
        first_out[...] = mean[...]
        second_out[...] = square[...]

    @pl.when(j >= blocks)
    def _():
        adam(first_far, second_far)

    direction = mean[...] / (1.0 - 0.9**10) / (jnp.sqrt(square[...] / (1.0 - 0.999**10)) + 1e-08)
    hi, lo = split(direction)
    hi, lo = hi.T, lo.T
    for i in range(count // tile):
        at = pl.ds(i * tile, tile)
        a_hi = basis_hi[at, :]
        step_out[at, :] = dot(a_hi, hi) + (dot(a_hi, lo) + dot(basis_lo[at, :], hi))


def body(replicas, shards, acts, cotangents, basis_old, moment_first, moment_second):
    tokens, features = acts.shape
    outs = cotangents.shape[1]
    rows = outs // shards
    rank = basis_old.shape[1]
    least = min(rows, features)
    pieces = 1 if least // replicas % 8 == 0 else 2
    blocks = BLOCKS
    while blocks > 1 and least * pieces // (replicas * blocks) % 8:
        blocks //= 2
    width = rank // pieces
    most = max(rows, features) * pieces
    vmem = pl.BlockSpec(memory_space=pltpu.VMEM)
    hbm = pl.BlockSpec(memory_space=pltpu.HBM)
    sizes = [size for _, size in stages(replicas, False)]
    links = max(sizes)
    slots = 3 * blocks
    sem = pltpu.SemaphoreType.DMA
    receive, length = [], most // blocks
    for size in sizes:
        length //= size
        receive.append(pltpu.VMEM((slots, max(size - 1, 1), length, width), F32))
    far = (max(shards - 1, 1) * rows, rank)
    power, mix, q_all, first_all, second_all = pl.pallas_call(
        functools.partial(reduce_kernel, replicas, shards, pieces, blocks),
        out_shape=[
            jax.ShapeDtypeStruct((features * pieces, width), F32),
            jax.ShapeDtypeStruct((rank, rank), F32),
            jax.ShapeDtypeStruct((outs * pieces, width), F32),
            jax.ShapeDtypeStruct(far, F32),
            jax.ShapeDtypeStruct(far, F32),
        ],
        in_specs=[hbm] * 5,
        out_specs=[vmem] * 3 + [hbm] * 2,
        scratch_shapes=[
            pltpu.VMEM((tokens, features), BF16),
            pltpu.VMEM((tokens, outs), BF16),
            pltpu.VMEM((features, rank), F32),
            pltpu.VMEM((rows, tokens), BF16),
            pltpu.VMEM((features, tokens), BF16),
            pltpu.VMEM((most, width), F32),
            pltpu.VMEM((rows * pieces, width), F32),
            *receive,
            pltpu.VMEM((3, tokens, rank), F32),
            pltpu.VMEM((3, shards - 1, tokens, rank), F32),
            pltpu.VMEM((rank, rank), F32),
            pltpu.VMEM((shards - 1, rank, rank), F32),
            pltpu.VMEM((rank, rank), F32),
            pltpu.VMEM((rank, rank), F32),
            sem((3,)),
            sem((slots, 6, links)),
            sem((slots, 6, links)),
            sem((6, shards)),
            sem((6, shards)),
            sem((blocks, shards)),
            sem((blocks, shards)),
        ],
        compiler_params=pltpu.CompilerParams(
            collective_id=0, has_side_effects=True, vmem_limit_bytes=WHOLE_VMEM
        ),
    )(acts, cotangents, basis_old, moment_first, moment_second)
    if pieces > 1:
        power = power.reshape(pieces, features, width).transpose(1, 0, 2).reshape(features, rank)
        q_all = q_all.reshape(shards, pieces, rows, width).transpose(0, 2, 1, 3).reshape(outs, rank)

    tile = min(TILE, rows)
    blocks = rows // tile
    where = lax.axis_index("shard").astype(jnp.int32).reshape(1)

    def column(j, at):
        return (0, lax.rem(at[0] + lax.div(j, blocks), shards) * blocks + lax.rem(j, blocks))

    fixed = lambda j, at: (0, 0)
    along = lambda j, at: (j, 0)
    early = lambda j, at: (jnp.minimum(j, blocks - 1), 0)
    late = lambda j, at: (jnp.maximum(j - blocks, 0), 0)
    return pl.pallas_call(
        functools.partial(finish_kernel, blocks),
        out_shape=[
            jax.ShapeDtypeStruct((features, outs), F32),
            jax.ShapeDtypeStruct((features, rank), F32),
            jax.ShapeDtypeStruct((rows, rank), F32),
            jax.ShapeDtypeStruct((rows, rank), F32),
        ],
        grid_spec=pltpu.PrefetchScalarGridSpec(
            num_scalar_prefetch=1,
            grid=(outs // tile,),
            in_specs=[
                pl.BlockSpec((features, rank), fixed),
                pl.BlockSpec((rank, rank), fixed),
                pl.BlockSpec((tile, rank), along),
                pl.BlockSpec((tile, rank), early),
                pl.BlockSpec((tile, rank), early),
                pl.BlockSpec((tile, rank), late),
                pl.BlockSpec((tile, rank), late),
            ],
            out_specs=[
                pl.BlockSpec((features, tile), column),
                pl.BlockSpec((features, rank), fixed),
                pl.BlockSpec((tile, rank), early),
                pl.BlockSpec((tile, rank), early),
            ],
            scratch_shapes=[
                pltpu.VMEM((features, rank), BF16),
                pltpu.VMEM((features, rank), BF16),
                pltpu.VMEM((tile, rank), F32),
                pltpu.VMEM((tile, rank), F32),
            ],
        ),
        compiler_params=pltpu.CompilerParams(vmem_limit_bytes=WHOLE_VMEM),
    )(where, power, mix, q_all, moment_first, moment_second, first_all, second_all)


def solution(mesh):
    placed = (P("dp", "shard"), P("dp", None), P("shard", None), P("shard", None), P("shard", None))
    return jax.shard_map(
        functools.partial(body, mesh.shape["dp"], mesh.shape["shard"]),
        mesh=mesh,
        in_specs=placed,
        out_specs=(P("shard", None), P("shard", None), P("shard", None), P("shard", None)),
        check_vma=False,
    )
```

time: 499 us -> 129 us (0.26); the launches traced: 492 us -> 129 us
  waiting for transfers between devices: 404 us -> 0 us
  Pallas kernels: 0 us -> 128 us
  matrix products: 62.5 us -> 0 us
  between operations: 15.4 us -> 0.64 us
  other arithmetic: 5.14 us -> 0 us
    psum x4 -> x0, waiting for transfers between devices: 383 us -> none  [the longest x1 136 us: body(): lax.psum(jnp.dot(grad_part, basis_old, precision=highest), ('dp', 'shard'))]
    pallas_call x0 -> x2, Pallas kernels: none -> 128 us  [the longest x1 114 us: body(): pl.pallas_call(functools.partial(reduce_kernel, replicas, shards, pieces,...]
    dot_general x19 -> x0, matrix products: 62.5 us -> none  [the longest x1 17.1 us: body(): power_part = jnp.dot(grad_part.T, image, precision=highest)]
    reduce_scatter x1 -> x0, waiting for transfers between devices: 10.9 us -> none  [body(): lax.psum_scatter(jnp.dot(grad_part, ortho, precision=highest), 'shard', s...]
    all_gather x1 -> x0, waiting for transfers between devices: 9.8 us -> none  [body(): lax.all_gather(direction, 'shard', axis=0, tiled=True)]
  transfers between devices with their start and end apart: 6 -> 0, of which waited for: 6 -> 0; matrix products, arithmetic and copies ran while one was open for 0% -> 0% of each run, Pallas kernels for 0% -> 0%
where the time goes in v2:
time: 129 us
  Pallas kernels  128 us (99%)
    pallas_call x1, Pallas kernels, body(): pl.pallas_call(functools.partial(reduce_kernel, replicas, shards, pieces,...  114 us
    pallas_call x1, Pallas kernels, body(): pl.pallas_call(functools.partial(finish_kernel, blocks), out_shape=[jax.S...  13.8 us

profile of v2, /device:TPU:0, one launch (start us, length us, event | category | flops | bytes accessed | tf_op | source)
XLA Modules:
  0.0 128.7 jit_solution(10019108238763833386)
XLA Ops:
  0.6 114.2 %shard_map.84 = (f32[1024,256]{1,0:T(8,128)}, f32[256,256]{1,0:T(8,128)}, f32[2048,256]{1,0:T(8,128)}, f32[1024,256]{1,0:T(8,128)}, f32[1024,256]{1,0:T(8,128)}) custom-call(bf16[256,1024]{1,0:T(8,128)(2,1)} %acts_in.1, bf16[256,2048]{1,0:T(8,128)(2,1)} %cot_in.1, f32[1024,256]{1,0:T(8,128)} %basis_in.1, f32[1024,256]{1,0:T(8,128)} %first.3, f32[1024,256]{1,0:T(8,128)} %second.3), custom_call_target="tpu_custom_call" | custom-call | tf_op jit(solution)/shard_map/pallas_call | solution.py:363
  114.9 13.8 %shard_map.85 = (f32[1024,2048]{1,0:T(8,128)}, f32[1024,256]{1,0:T(8,128)}, f32[1024,256]{1,0:T(8,128)}, f32[1024,256]{1,0:T(8,128)}) custom-call(s32[1]{0:T(128)} %bitcast.where, f32[1024,256]{1,0:T(8,128)} %get-tuple-element.9.power, f32[256,256]{1,0:T(8,128)} %get-tuple-element.10.mix, f32[2048,256]{1,0:T(8,128)} %get-tuple-element.11.q, ...), custom_call_target="tpu_custom_call" | custom-call | tf_op jit(solution)/shard_map/pallas_call | solution.py:416

commit v3 on v2

--- a/solution.py
+++ b/solution.py
@@ -12,7 +12,9 @@
 F32 = jnp.float32
 BF16 = jnp.bfloat16
 TILE = 256
-BLOCKS = 4
+ORDER = ("line", "plane", "plane", "plane")
+BLOCKS = len(ORDER)
+GREET = "plane"
 WHOLE_VMEM = 62 * 2**20
 
 
@@ -31,21 +33,28 @@
     return dot(a_hi, b_hi, dims) + (dot(a_hi, b_lo, dims) + dot(a_lo, b_hi, dims))
 
 
-def stages(replicas, odd):
+def stages(replicas, kind):
     pairs, stride, left = [], 1, replicas
     while left % 2 == 0 and len(pairs) < 2:
         pairs.append((stride, 2))
         stride, left = stride * 2, left // 2
-    if odd:
-        pairs = pairs[::-1]
-    return pairs + [(stride, left)]
+    line = [(stride, left)]
+    if kind == "plane":
+        return [(1, stride)] + line
+    if kind == "line":
+        return line + [(1, stride)]
+    if kind == "yx":
+        return pairs[::-1] + line
+    if kind == "zxy":
+        return line + pairs
+    return pairs + line
 
 
 def reduce_kernel(
     replicas, shards, pieces, blocks,
     acts_in, cot_in, basis_in, first, second,
     power, mix, q_all, first_all, second_all,
-    acts, cot, basis, cot_t, acts_t, part, image, recv_a, recv_b, recv_c, tok, tok_recv, gram, gram_recv, ns_g, ns_t,
+    acts, cot, basis, cot_t, acts_t, part, image, received, tok, tok_recv, gram, gram_recv, ns_g, ns_t,
     load_sem, dp_send, dp_recv, sh_send, sh_recv, fwd_send, fwd_recv,
 ):
     me = lax.axis_index("dp")
@@ -55,7 +64,6 @@
     rank = basis.shape[1]
     width = rank // pieces
     inverse = 1.0 / math.sqrt(tokens * replicas)
-    receive = (recv_a, recv_b, recv_c)
     mesh_id = pl.DeviceIdType.MESH
 
     loads = [
@@ -86,7 +94,7 @@
 
     barrier = pltpu.get_barrier_semaphore()
     greeted = 0
-    for stride, size in stages(replicas, False):
+    for stride, size in stages(replicas, GREET):
         for k in range(1, size):
             pl.semaphore_signal(barrier, inc=1, device_id=(peer(stride, size, k), own), device_id_type=mesh_id)
             greeted += 1
@@ -125,17 +133,17 @@
         else:
             out[...] += value
 
-    def exchange(index, buffer, received):
+    def exchange(index, buffer, target):
         return [
-            remote(buffer, received.at[k - 1], sh_send.at[index, k - 1], sh_recv.at[index, k - 1], to_shard(k))
+            remote(buffer, target.at[k - 1], sh_send.at[index, k - 1], sh_recv.at[index, k - 1], to_shard(k))
             for k in range(1, shards)
         ]
 
-    def total(copies, buffer, received):
+    def total(copies, buffer, arrived):
         value = buffer[...]
         for k, copy in enumerate(copies):
             copy.wait()
-            value = value + received[k]
+            value = value + arrived[k]
         return value
 
     def piece(index, h, count, left, hi, lo, full, consume):
@@ -150,14 +158,16 @@
 
         tiles(h * (count // blocks), count // blocks, expand)
         slot = index * blocks + h
-        path = stages(replicas, h % 2 == 1)
+        path = stages(replicas, ORDER[h])
+        store = slot * length
         for stage, (stride, size) in enumerate(path):
             chunk = length // size
             at = place(stride, size)
+            here = store
             copies = [
                 remote(
                     part.at[pl.ds(pl.multiple_of(base + lax.rem(at + k, size) * chunk, 8), chunk), :],
-                    receive[stage].at[slot, k - 1],
+                    received.at[pl.ds(here + (k - 1) * chunk, chunk), :],
                     dp_send.at[slot, stage, k - 1], dp_recv.at[slot, stage, k - 1], (peer(stride, size, k), own),
                 )
                 for k in range(1, size)
@@ -168,7 +178,8 @@
             value = part[pl.ds(base, chunk), :]
             for k, copy in enumerate(copies):
                 copy.wait()
-                value = value + receive[stage][slot, k]
+                value = value + received[pl.ds(here + k * chunk, chunk), :]
+            store = store + (size - 1) * chunk
             if stage + 1 < len(path):
                 part[pl.ds(base, chunk), :] = value
             else:
@@ -351,14 +362,9 @@
     most = max(rows, features) * pieces
     vmem = pl.BlockSpec(memory_space=pltpu.VMEM)
     hbm = pl.BlockSpec(memory_space=pltpu.HBM)
-    sizes = [size for _, size in stages(replicas, False)]
-    links = max(sizes)
+    links = max(size for _, size in stages(replicas, "plane"))
     slots = 3 * blocks
     sem = pltpu.SemaphoreType.DMA
-    receive, length = [], most // blocks
-    for size in sizes:
-        length //= size
-        receive.append(pltpu.VMEM((slots, max(size - 1, 1), length, width), F32))
     far = (max(shards - 1, 1) * rows, rank)
     power, mix, q_all, first_all, second_all = pl.pallas_call(
         functools.partial(reduce_kernel, replicas, shards, pieces, blocks),
@@ -379,7 +385,7 @@
             pltpu.VMEM((features, tokens), BF16),
             pltpu.VMEM((most, width), F32),
             pltpu.VMEM((rows * pieces, width), F32),
-            *receive,
+            pltpu.VMEM((3 * most, width), F32),
             pltpu.VMEM((3, tokens, rank), F32),
             pltpu.VMEM((3, shards - 1, tokens, rank), F32),
             pltpu.VMEM((rank, rank), F32),

time: 129 us -> 114 us (0.88)
  Pallas kernels: 128 us -> 113 us
    pallas_call x1, Pallas kernels: 114 us -> 98.9 us  [body(): pl.pallas_call(functools.partial(reduce_kernel, replicas, shards, pieces,...]
where the time goes in v3:
time: 114 us; the launch traced here: 113 us
  Pallas kernels  113 us (99%)
    pallas_call x1, Pallas kernels, body(): pl.pallas_call(functools.partial(reduce_kernel, replicas, shards, pieces,...  98.9 us
    pallas_call x1, Pallas kernels, body(): pl.pallas_call(functools.partial(finish_kernel, blocks), out_shape=[jax.S...  13.8 us

profile of v3, /device:TPU:0, one launch (start us, length us, event | category | flops | bytes accessed | tf_op | source)
XLA Modules:
  0.0 113.3 jit_solution(10080339605877945705)
XLA Ops:
  0.6 98.9 %shard_map.84 = (f32[1024,256]{1,0:T(8,128)}, f32[256,256]{1,0:T(8,128)}, f32[2048,256]{1,0:T(8,128)}, f32[1024,256]{1,0:T(8,128)}, f32[1024,256]{1,0:T(8,128)}) custom-call(bf16[256,1024]{1,0:T(8,128)(2,1)} %acts_in.1, bf16[256,2048]{1,0:T(8,128)(2,1)} %cot_in.1, f32[1024,256]{1,0:T(8,128)} %basis_in.1, f32[1024,256]{1,0:T(8,128)} %first.3, f32[1024,256]{1,0:T(8,128)} %second.3), custom_call_target="tpu_custom_call" | custom-call | tf_op jit(solution)/shard_map/pallas_call | solution.py:369
  99.5 13.8 %shard_map.85 = (f32[1024,2048]{1,0:T(8,128)}, f32[1024,256]{1,0:T(8,128)}, f32[1024,256]{1,0:T(8,128)}, f32[1024,256]{1,0:T(8,128)}) custom-call(s32[1]{0:T(128)} %bitcast.where, f32[1024,256]{1,0:T(8,128)} %get-tuple-element.9.power, f32[256,256]{1,0:T(8,128)} %get-tuple-element.10.mix, f32[2048,256]{1,0:T(8,128)} %get-tuple-element.11.q, ...), custom_call_target="tpu_custom_call" | custom-call | tf_op jit(solution)/shard_map/pallas_call | solution.py:422

commit v4 on v3

--- a/solution.py
+++ b/solution.py
@@ -408,7 +408,7 @@
         power = power.reshape(pieces, features, width).transpose(1, 0, 2).reshape(features, rank)
         q_all = q_all.reshape(shards, pieces, rows, width).transpose(0, 2, 1, 3).reshape(outs, rank)
 
-    tile = min(TILE, rows)
+    tile = min(2 * TILE, rows)
     blocks = rows // tile
     where = lax.axis_index("shard").astype(jnp.int32).reshape(1)
 

time: 114 us -> 112 us (0.982)
  no operation moved by 1% of the time
where the time goes in v4:
time: 112 us
  Pallas kernels  112 us (100%)
    pallas_call x1, Pallas kernels, body(): pl.pallas_call(functools.partial(reduce_kernel, replicas, shards, pieces,...  98.9 us
    pallas_call x1, Pallas kernels, body(): pl.pallas_call(functools.partial(finish_kernel, blocks), out_shape=[jax.S...  12.7 us

profile of v4, /device:TPU:0, one launch (start us, length us, event | category | flops | bytes accessed | tf_op | source)
XLA Modules:
  0.0 112.2 jit_solution(17915400760160381979)
XLA Ops:
  0.6 98.9 %shard_map.84 = (f32[1024,256]{1,0:T(8,128)}, f32[256,256]{1,0:T(8,128)}, f32[2048,256]{1,0:T(8,128)}, f32[1024,256]{1,0:T(8,128)}, f32[1024,256]{1,0:T(8,128)}) custom-call(bf16[256,1024]{1,0:T(8,128)(2,1)} %acts_in.1, bf16[256,2048]{1,0:T(8,128)(2,1)} %cot_in.1, f32[1024,256]{1,0:T(8,128)} %basis_in.1, f32[1024,256]{1,0:T(8,128)} %first.3, f32[1024,256]{1,0:T(8,128)} %second.3), custom_call_target="tpu_custom_call" | custom-call | tf_op jit(solution)/shard_map/pallas_call | solution.py:369
  99.5 12.7 %shard_map.85 = (f32[1024,2048]{1,0:T(8,128)}, f32[1024,256]{1,0:T(8,128)}, f32[1024,256]{1,0:T(8,128)}, f32[1024,256]{1,0:T(8,128)}) custom-call(s32[1]{0:T(128)} %bitcast.where, f32[1024,256]{1,0:T(8,128)} %get-tuple-element.9.power, f32[256,256]{1,0:T(8,128)} %get-tuple-element.10.mix, f32[2048,256]{1,0:T(8,128)} %get-tuple-element.11.q, ...), custom_call_target="tpu_custom_call" | custom-call | tf_op jit(solution)/shard_map/pallas_call | solution.py:422
